TPU v7x, 256 devices: a whole 4x4x8 slice. The times are simulated.
256 devices in a mesh: section: 8 (over z), expert: 32 (over x, y, core).
Axes of the slice: x: 4, y: 4, z: 8, core: 2. Of those that a mesh axis runs over, the one named last changes fastest.
Arguments:
- grad_out: bfloat16 [4096, 4096], P('expert', 'section'), may hold values from -6 to 6
- probs: float32 [4096, 8], P('expert'), may hold values from 0.05 to 0.4
- expert_ids: int32 [4096, 8], P('expert'), may hold values from 0 to 63, all different within a row; in each aligned block of 128 rows (0 to 127, 128 to 255, ...) at most 24 rows name the same one
- w_gate: bfloat16 [64, 1536, 4096], P('expert', 'section'), may hold values from -0.09375 to 0.09375
- w_up: bfloat16 [64, 1536, 4096], P('expert', 'section'), may hold values from -0.09375 to 0.09375
- w_down: bfloat16 [64, 1536, 4096], P('expert', 'section'), may hold values from -0.15625 to 0.15625
- saved_gate: bfloat16 [64, 1536, 768], P('expert', 'section'), may hold values from -3 to 3
- saved_up: bfloat16 [64, 1536, 768], P('expert', 'section'), may hold values from -3 to 3
Outputs:
- grad_in: bfloat16 [4096, 4096], P('expert', 'section')
- grad_probs: bfloat16 [4096, 8], P('expert')
Inputs may be any that keep to these rules, and one draw needn't show every extreme that they name: `expert_ids`: each token names 8 different experts. Within the tokens of one index of expert (aligned blocks of 128 tokens) no expert is named more than 24 times, a bound that some block reaches.
All inputs are finite; a program needn't handle non-finite values.
Results may differ from a plain program's by a relative error of at most 0.015.
Values may be sent and summed in bfloat16 or wider, within the bound.
A program may use at most 128 MiB of HBM per device.

v0:
```python
import jax
import jax.numpy as jnp
from jax import lax
from jax.sharding import PartitionSpec as P

TOPK = 8


def local(grad_out, probs, expert_ids, w_gate, w_up, w_down, saved_gate, saved_up):
    groups = lax.axis_size("expert")
    local_experts = w_gate.shape[0]
    expert_count = local_experts * groups
    slot_count = saved_gate.shape[2]
    capacity = slot_count // groups
    token_count = grad_out.shape[0]
    feature_share = grad_out.shape[1]
    picked = expert_ids.reshape(-1)
    onehot = (picked[:, None] == jnp.arange(expert_count, dtype=jnp.int32)[None, :]).astype(
        jnp.int32
    )
    before = jnp.cumsum(onehot, axis=0) - onehot
    position = jnp.sum(before * onehot, axis=1)
    slot = picked * capacity + position
    owner = jnp.arange(picked.shape[0], dtype=jnp.int32) // TOPK
    table = jnp.full((expert_count * capacity,), token_count, jnp.int32).at[slot].set(owner)
    full_rows = lax.all_gather(grad_out, "section", axis=1, tiled=True)
    padded = jnp.concatenate([full_rows, jnp.zeros((1, full_rows.shape[1]), jnp.bfloat16)], axis=0)
    outgoing = padded[table].reshape(expert_count, capacity, full_rows.shape[1])
    arrived = lax.all_to_all(outgoing, "expert", split_axis=0, concat_axis=1, tiled=True)
    hidden_grad = jnp.einsum("esd,efd->efs", arrived, w_down, preferred_element_type=jnp.float32)
    gate_act = saved_gate.astype(jnp.float32)
    up_act = saved_up.astype(jnp.float32)
    sigmoid_gate = jax.nn.sigmoid(gate_act)
    silu_gate = gate_act * sigmoid_gate
    router_part = jnp.sum(silu_gate * up_act * hidden_grad, axis=1)
    router_grad = lax.psum(router_part, "section").astype(jnp.bfloat16)
    gate_grad = (
        hidden_grad * up_act * sigmoid_gate * (1.0 + gate_act * (1.0 - sigmoid_gate))
    ).astype(jnp.bfloat16)
    up_grad = (hidden_grad * silu_gate).astype(jnp.bfloat16)
    term = jnp.einsum("efc,efs->esc", w_gate, gate_grad, preferred_element_type=jnp.float32)
    term = term + jnp.einsum("efc,efs->esc", w_up, up_grad, preferred_element_type=jnp.float32)
    shares = lax.psum_scatter(term.astype(jnp.bfloat16), "section", scatter_dimension=2, tiled=True)
    back_grad, back_router = (
        lax.all_to_all(shares, "expert", split_axis=1, concat_axis=0, tiled=True),
        lax.all_to_all(router_grad, "expert", split_axis=1, concat_axis=0, tiled=True),
    )
    rows = back_grad.reshape(expert_count * capacity, feature_share)[slot]
    weighted = (
        rows.astype(jnp.float32).reshape(token_count, TOPK, feature_share) * probs[:, :, None]
    )
    grad_in = jnp.sum(weighted, axis=1).astype(jnp.bfloat16)
    grad_probs = back_router.reshape(-1)[slot].reshape(token_count, TOPK)
    return (grad_in, grad_probs)


def solution(mesh):
    placed = (
        P("expert", "section"),
        P("expert", None),
        P("expert", None),
        P("expert", "section", None),
        P("expert", "section", None),
        P("expert", "section", None),
        P("expert", "section", None),
        P("expert", "section", None),
    )
    return jax.shard_map(
        local,
        mesh=mesh,
        in_specs=placed,
        out_specs=(P("expert", "section"), P("expert", None)),
        check_vma=False,
    )
```

profile of v0, /device:TPU:1, one launch (start us, length us, event | category | flops | bytes accessed | tf_op | source)
XLA Modules:
  0.0 454.7 jit_solution(9075502163950577890)
XLA Ops:
  7.2 0.7 all-gather.2.cloned.1.call-update
  8.0 0.9 copy.23
  9.1 0.7 fusion.16
  9.8 30.8 %reduce-window.6 = s32[64,8,128]{2,1,0:T(8,128)S(1)} reduce-window(s32[64,8,128]{2,1,0:T(8,128)} %fusion.16, s32[]{:T(128)} %constant.30.clone.1), window={size=1x1x128 pad=0_0x0_0x127_0}, to_apply=%region_0.0 | reduce-window | flops 8323072 | bytes 524292 | tf_op jit(solution)/shard_map/reduce-window
  40.7 0.9 slice.14
  41.5 1.1 copy.25
  42.7 0.1 copy.22
  42.9 0.1 mul.53
  43.0 0.1 broadcast_add_fusion
  43.2 4.3 scatter_custom_fusion
  47.6 2.4 concatenate.3
  50.0 23.4 %gather_fusion = bf16[1536,4096]{1,0:T(8,128)(2,1)} fusion(bf16[129,4096]{1,0:T(8,128)(2,1)} %concatenate.3, s32[2048]{0:T(1024)S(1)} %pad_clamp_fusion), kind=kCustom, calls=%fused_computation | custom fusion | bytes 25171968 | tf_op jit(solution)/shard_map/gather | solution.py:28
  73.4 152.6 %all_to_all.49 = bf16[64,24,4096]{2,1,0:T(8,128)(2,1)S(1)} all-to-all(bf16[64,24,4096]{2,1,0:T(8,128)(2,1)} %bitcast.40), channel_id=1, replica_groups=mesh['section'=8,'expert'=32] {'expert'}, dimensions={0} | all-to-all | bytes 25165824 | tf_op jit(solution)/shard_map/all_to_all | solution.py:29
  226.0 5.2 %copy.27 = bf16[2,32,24,4096]{3,2,1,0:T(8,128)(2,1)} copy(bf16[2,32,24,4096]{3,2,0,1:T(8,128)(2,1)S(1)} %bitcast.41) | data formatting | bytes 25165824 | tf_op jit(solution)/shard_map/all_to_all | solution.py:29
  231.1 11.1 %fusion.5 = (f32[2,768]{1,0:T(2,128)S(1)}, f32[2,192,768]{2,1,0:T(8,128)}) fusion(bf16[2,192,768]{2,1,0:T(8,128)(2,1)} %param.15, bf16[2,192,768]{2,1,0:T(8,128)(2,1)} %param.14, bf16[2,768,4096]{2,1,0:T(8,128)(2,1)} %bitcast.42, bf16[2,192,4096]{2,1,0:T(8,128)(2,1)} %param.13), kind=kOutput, calls=%fused_computation.17 | convolution fusion | flops 2418571776 | bytes 18094080 | tf_op jit(solution)/shard_map/esd,efd->efs/dot_general | solution.py:30
  242.2 11.8 %fusion.10 = f32[2,768,4096]{2,1,0:T(8,128)} fusion(bf16[2,192,4096]{2,1,0:T(8,128)(2,1)S(1)} %copy-done, f32[2,192,768]{2,1,0:T(8,128)} %get-tuple-element.7, bf16[2,192,768]{2,1,0:T(8,128)(2,1)} %param.15, bf16[2,192,768]{2,1,0:T(8,128)(2,1)} %param.14), kind=kOutput, calls=%fused_computation.23 | convolution fusion | flops 2419458048 | bytes 30670848 | tf_op jit(solution)/shard_map/efc,efs->esc/dot_general | solution.py:41
  254.1 16.5 %add_convert_fusion = bf16[2,768,4096]{2,1,0:T(8,128)(2,1)} fusion(f32[2,768,4096]{2,1,0:T(8,128)} %fusion.10, bf16[2,192,4096]{2,1,0:T(8,128)(2,1)} %param.12, f32[2,192,768]{2,1,0:T(8,128)} %get-tuple-element.7, bf16[2,192,768]{2,1,0:T(8,128)(2,1)} %param.14), kind=kOutput, calls=%fused_computation.4 | convolution fusion | flops 2430566400 | bytes 42663936 | tf_op jit(solution)/shard_map/efc,efs->esc/dot_general | solution.py:42
  270.6 14.2 %psum.7 = bf16[2,768]{1,0:T(2,128)(2,1)S(1)} all-reduce(f32[2,768]{1,0:T(2,128)S(1)} %get-tuple-element.6), channel_id=1, replica_groups=mesh['section'=8,'expert'=32] {'section'}, use_global_device_ids=true, to_apply=%region_7.8 | all-reduce | flops 1536 | bytes 9216 | tf_op jit(solution)/shard_map/psum | solution.py:36
  284.8 0.1 all_to_all.43
  284.9 0.6 copy.31
  285.5 6.8 %all-to-all-start.2 = ((bf16[2,32,24]{2,0,1:T(2,128)(2,1)}), bf16[2,32,24]{2,0,1:T(2,128)(2,1)S(1)}, u32[]{:S(2)}, u32[]{:S(2)}) async-start(bf16[2,32,24]{2,0,1:T(2,128)(2,1)} %copy.31), calls=%async_computation.3 | async-start | bytes 32768 | tf_op jit(solution)/shard_map/all_to_all | solution.py:46
  292.3 108.8 %reduce-scatter.2.cloned.1.call-done = bf16[2,768,512]{2,1,0:T(8,128)(2,1)} async-done(((bf16[2,768,4096]{2,1,0:T(8,128)(2,1)}), bf16[2,768,512]{2,1,0:T(8,128)(2,1)}) %reduce-scatter.2.cloned.1.call-update) | async-done | bytes 1572880 | tf_op jit(solution)/shard_map/reduce_scatter | solution.py:43
  401.1 4.2 copy.28
  405.3 7.6 %all-to-all-start.1 = ((bf16[2,768,512]{2,0,1:T(2,128)(2,1)}), bf16[2,768,512]{2,0,1:T(2,128)(2,1)}, u32[]{:S(2)}, u32[]{:S(2)}) async-start(bf16[2,768,512]{2,0,1:T(2,128)(2,1)} %copy.28), calls=%async_computation.2 | async-start | bytes 3145728 | tf_op jit(solution)/shard_map/all_to_all | solution.py:45
  412.9 0.1 copy.30
  413.0 0.1 reshape.75
  413.1 6.8 %gather_fusion.2 = bf16[1024]{0:T(1024)(128)(2,1)S(1)} fusion(bf16[1536]{0:T(1024)(128)(2,1)S(1)} %reshape.75, s32[1024]{0:T(1024)S(1)} %broadcast_clamp_fusion), kind=kCustom, calls=%fused_computation.2 | custom fusion | bytes 8192 | tf_op jit(solution)/shard_map/gather | solution.py:53
  420.0 0.7 copy.32
  420.7 14.9 %all-to-all-done.1 = bf16[2,768,512]{2,0,1:T(2,128)(2,1)} async-done(((bf16[2,768,512]{2,0,1:T(2,128)(2,1)}), bf16[2,768,512]{2,0,1:T(2,128)(2,1)}, u32[]{:S(2)}, u32[]{:S(2)}) %all-to-all-start.1) | async-done | bytes 1572896 | tf_op jit(solution)/shard_map/all_to_all | solution.py:45
  435.6 2.9 copy.29
  438.5 6.7 %gather_fusion.1 = bf16[1024,512]{1,0:T(8,128)(2,1)} fusion(bf16[1536,512]{1,0:T(8,128)(2,1)} %bitcast.39, s32[1024]{0:T(1024)S(1)} %broadcast_clamp_fusion), kind=kCustom, calls=%fused_computation.1 | custom fusion | bytes 2101248 | tf_op jit(solution)/shard_map/gather | solution.py:48
  445.2 2.6 fusion
  (24 shorter events, 0.6 us)
Async XLA Ops:
  7.2 235.1 %copy-start = (bf16[2,192,4096]{2,1,0:T(8,128)(2,1)S(1)}, bf16[2,192,4096]{2,1,0:T(8,128)(2,1)}, u32[]{:S(2)}) copy-start(bf16[2,192,4096]{2,1,0:T(8,128)(2,1)} %param.11) | copy-start | bytes 9437188
  7.2 35.6 %copy-start.1 = (s32[128,8]{0,1:T(8,128)S(1)}, s32[128,8]{0,1:T(8,128)}, u32[]{:S(2)}) copy-start(s32[128,8]{0,1:T(8,128)} %param.10) | copy-start | bytes 12292
  7.2 40.4 %all-gather.2.cloned.1.call-start = ((), (), s32[]{:S(2)}) async-start(), calls=%async_computation.4 | async-start | bytes 1179648 | tf_op jit(solution)/shard_map/all_gather | solution.py:26
  7.9 393.2 %reduce-scatter.2.cloned.1.call-start = ((), (), s32[]{:S(2)}) async-start(), calls=%async_computation.5 | async-start | bytes 14155776 | tf_op jit(solution)/shard_map/reduce_scatter | solution.py:43
  285.5 119.8 %all-to-all-start.2 = ((bf16[2,32,24]{2,0,1:T(2,128)(2,1)}), bf16[2,32,24]{2,0,1:T(2,128)(2,1)S(1)}, u32[]{:S(2)}, u32[]{:S(2)}) async-start(bf16[2,32,24]{2,0,1:T(2,128)(2,1)} %copy.31), calls=%async_computation.3 | async-start | bytes 32768 | tf_op jit(solution)/shard_map/all_to_all | solution.py:46
  405.3 7.6 %copy-start.2 = (f32[128,8]{0,1:T(8,128)S(1)}, f32[128,8]{0,1:T(8,128)}, u32[]{:S(2)}) copy-start(f32[128,8]{0,1:T(8,128)} %param.9) | copy-start | bytes 12292
  405.3 30.3 %all-to-all-start.1 = ((bf16[2,768,512]{2,0,1:T(2,128)(2,1)}), bf16[2,768,512]{2,0,1:T(2,128)(2,1)}, u32[]{:S(2)}, u32[]{:S(2)}) async-start(bf16[2,768,512]{2,0,1:T(2,128)(2,1)} %copy.28), calls=%async_computation.2 | async-start | bytes 3145728 | tf_op jit(solution)/shard_map/all_to_all | solution.py:45
Sparse Core Ops, SparseCore 0:
  9.8 37.5 all-gather.1
  270.7 130.3 reduce-scatter.1
where the time goes:
time: 457 us; the launch traced here: 455 us
  blocking collectives  167 us (37%)
  waiting for transfers between devices  124 us (27%)
  local copies, waits for them, and re-layouts  60.9 us (13%)
  matrix products  39.4 us (9%)
  other arithmetic  34.4 us (8%)
  starting transfers between devices  14.5 us (3%)
  between operations  14.2 us (3%)
    all_to_all x1, blocking collectives, local(): lax.all_to_all(outgoing, 'expert', split_axis=0, concat_axis=1, tiled=True)  153 us
    reduce_scatter x1, waiting for transfers between devices, local(): lax.psum_scatter(term.astype(jnp.bfloat16), 'section', scatter_dimension=...  109 us
    another operation x3, other arithmetic  31 us
    gather x1, local copies, waits for them, and re-layouts, local(): outgoing = padded[table].reshape(expert_count, capacity, full_rows.shape[1])  23.4 us
    dot_general x1, matrix products, local(): jnp.einsum('efc,efs->esc', w_up, up_grad, preferred_element_type=jnp.floa...  16.5 us
    all_to_all x1, waiting for transfers between devices, local(): lax.all_to_all(shares, 'expert', split_axis=1, concat_axis=0, tiled=True)  14.9 us
    psum x1, blocking collectives, local(): router_grad = lax.psum(router_part, 'section').astype(jnp.bfloat16)  14.2 us
    dot_general x1, matrix products, local(): jnp.einsum('efc,efs->esc', w_gate, gate_grad, preferred_element_type=jnp....  11.8 us
  transfers between devices with their start and end apart: 4, of which 2 were waited for; matrix products, arithmetic and copies ran while one was open for 11% of the time, Pallas kernels for 0%

commit v1 on v0

--- a/solution.py
+++ b/solution.py
@@ -33,7 +33,7 @@
     sigmoid_gate = jax.nn.sigmoid(gate_act)
     silu_gate = gate_act * sigmoid_gate
     router_part = jnp.sum(silu_gate * up_act * hidden_grad, axis=1)
-    router_grad = lax.psum(router_part, "section").astype(jnp.bfloat16)
+    router_grad = jnp.sum(jax.lax.all_gather(router_part, "section"), axis=0).astype(jnp.bfloat16)
     gate_grad = (
         hidden_grad * up_act * sigmoid_gate * (1.0 + gate_act * (1.0 - sigmoid_gate))
     ).astype(jnp.bfloat16)

time: 457 us -> 457 us (level)
  waiting for transfers between devices: 124 us -> 116 us
  blocking collectives: 167 us -> 173 us
    all_gather x0 -> x1, blocking collectives: none -> 20.6 us  [local(): jax.lax.all_gather(router_part, 'section')]
    psum x1 -> x0, blocking collectives: 14.2 us -> none  [local(): router_grad = lax.psum(router_part, 'section').astype(jnp.bfloat16)]
    reduce_scatter x1, waiting for transfers between devices: 109 us -> 101 us  [local(): lax.psum_scatter(term.astype(jnp.bfloat16), 'section', scatter_dimension=...]
where the time goes in v1:
time: 457 us; the launch traced here: 455 us
  blocking collectives  173 us (38%)
  waiting for transfers between devices  116 us (25%)
  local copies, waits for them, and re-layouts  60.9 us (13%)
  matrix products  39.4 us (9%)
  other arithmetic  34.5 us (8%)
  starting transfers between devices  16.5 us (4%)
  between operations  14.2 us (3%)
    all_to_all x1, blocking collectives, local(): lax.all_to_all(outgoing, 'expert', split_axis=0, concat_axis=1, tiled=True)  153 us
    reduce_scatter x1, waiting for transfers between devices, local(): lax.psum_scatter(term.astype(jnp.bfloat16), 'section', scatter_dimension=...  101 us
    another operation x3, other arithmetic  31 us
    gather x1, local copies, waits for them, and re-layouts, local(): outgoing = padded[table].reshape(expert_count, capacity, full_rows.shape[1])  23.4 us
    all_gather x1, blocking collectives, local(): jax.lax.all_gather(router_part, 'section')  20.6 us
    dot_general x1, matrix products, local(): jnp.einsum('efc,efs->esc', w_up, up_grad, preferred_element_type=jnp.floa...  16.5 us
    all_to_all x1, waiting for transfers between devices, local(): lax.all_to_all(shares, 'expert', split_axis=1, concat_axis=0, tiled=True)  14.9 us
    dot_general x1, matrix products, local(): jnp.einsum('efc,efs->esc', w_gate, gate_grad, preferred_element_type=jnp....  11.8 us
  transfers between devices with their start and end apart: 4, of which 2 were waited for; matrix products, arithmetic and copies ran while one was open for 11% of the time, Pallas kernels for 0%

profile of v1, /device:TPU:1, one launch (start us, length us, event | category | flops | bytes accessed | tf_op | source)
XLA Modules:
  0.0 454.8 jit_solution(803238514626940196)
XLA Ops:
  7.2 0.7 all-gather.4.cloned.1.call-update
  8.0 0.9 copy.23
  9.1 0.7 fusion.16
  9.8 30.8 %reduce-window.6 = s32[64,8,128]{2,1,0:T(8,128)S(1)} reduce-window(s32[64,8,128]{2,1,0:T(8,128)} %fusion.16, s32[]{:T(128)} %constant.30.clone.1), window={size=1x1x128 pad=0_0x0_0x127_0}, to_apply=%region_0.0 | reduce-window | flops 8323072 | bytes 524292 | tf_op jit(solution)/shard_map/reduce-window
  40.7 0.9 slice.14
  41.5 1.1 copy.25
  42.7 0.1 copy.22
  42.9 0.1 mul.53
  43.0 0.1 broadcast_add_fusion
  43.2 4.3 scatter_custom_fusion
  47.6 2.4 concatenate.3
  50.0 23.4 %gather_fusion = bf16[1536,4096]{1,0:T(8,128)(2,1)} fusion(bf16[129,4096]{1,0:T(8,128)(2,1)} %concatenate.3, s32[2048]{0:T(1024)S(1)} %pad_clamp_fusion), kind=kCustom, calls=%fused_computation | custom fusion | bytes 25171968 | tf_op jit(solution)/shard_map/gather | solution.py:28
  73.4 152.6 %all_to_all.46 = bf16[64,24,4096]{2,1,0:T(8,128)(2,1)S(1)} all-to-all(bf16[64,24,4096]{2,1,0:T(8,128)(2,1)} %bitcast.41), channel_id=1, replica_groups=mesh['section'=8,'expert'=32] {'expert'}, dimensions={0} | all-to-all | bytes 25165824 | tf_op jit(solution)/shard_map/all_to_all | solution.py:29
  226.0 5.2 %copy.27 = bf16[2,32,24,4096]{3,2,1,0:T(8,128)(2,1)} copy(bf16[2,32,24,4096]{3,2,0,1:T(8,128)(2,1)S(1)} %bitcast.42) | data formatting | bytes 25165824 | tf_op jit(solution)/shard_map/all_to_all | solution.py:29
  231.1 11.1 %fusion.5 = (f32[2,768]{1,0:T(2,128)S(1)}, f32[2,192,768]{2,1,0:T(8,128)}) fusion(bf16[2,192,768]{2,1,0:T(8,128)(2,1)} %param.15, bf16[2,192,768]{2,1,0:T(8,128)(2,1)} %param.14, bf16[2,768,4096]{2,1,0:T(8,128)(2,1)} %bitcast.43, bf16[2,192,4096]{2,1,0:T(8,128)(2,1)} %param.13), kind=kOutput, calls=%fused_computation.17 | convolution fusion | flops 2418571776 | bytes 18094080 | tf_op jit(solution)/shard_map/esd,efd->efs/dot_general | solution.py:30
  242.2 11.8 %fusion.10 = f32[2,768,4096]{2,1,0:T(8,128)} fusion(bf16[2,192,4096]{2,1,0:T(8,128)(2,1)S(1)} %copy-done, f32[2,192,768]{2,1,0:T(8,128)} %get-tuple-element.7, bf16[2,192,768]{2,1,0:T(8,128)(2,1)} %param.15, bf16[2,192,768]{2,1,0:T(8,128)(2,1)} %param.14), kind=kOutput, calls=%fused_computation.23 | convolution fusion | flops 2419458048 | bytes 30670848 | tf_op jit(solution)/shard_map/efc,efs->esc/dot_general | solution.py:41
  254.1 16.5 %add_convert_fusion = bf16[2,768,4096]{2,1,0:T(8,128)(2,1)} fusion(f32[2,768,4096]{2,1,0:T(8,128)} %fusion.10, bf16[2,192,4096]{2,1,0:T(8,128)(2,1)} %param.12, f32[2,192,768]{2,1,0:T(8,128)} %get-tuple-element.7, bf16[2,192,768]{2,1,0:T(8,128)(2,1)} %param.14), kind=kOutput, calls=%fused_computation.4 | convolution fusion | flops 2430566400 | bytes 42663936 | tf_op jit(solution)/shard_map/efc,efs->esc/dot_general | solution.py:42
  270.6 20.6 %all-gather.1 = f32[8,2,768]{2,1,0:T(2,128)S(1)} all-gather(f32[1,2,768]{2,1,0:T(2,128)S(1)} %bitcast.50), channel_id=2, replica_groups=mesh['section'=8,'expert'=32] {'section'}, dimensions={0}, use_global_device_ids=true | all-gather | bytes 55296 | tf_op jit(solution)/shard_map/all_gather | solution.py:36
  291.2 0.1 convert_element_type.50
  291.3 0.6 copy.31
  291.9 8.7 %all-to-all-start.2 = ((bf16[2,32,24]{2,0,1:T(2,128)(2,1)}), bf16[2,32,24]{2,0,1:T(2,128)(2,1)S(1)}, u32[]{:S(2)}, u32[]{:S(2)}) async-start(bf16[2,32,24]{2,0,1:T(2,128)(2,1)} %copy.31), calls=%async_computation.3 | async-start | bytes 32768 | tf_op jit(solution)/shard_map/all_to_all | solution.py:46
  300.7 100.6 %reduce-scatter.2.cloned.1.call-done = bf16[2,768,512]{2,1,0:T(8,128)(2,1)} async-done(((bf16[2,768,4096]{2,1,0:T(8,128)(2,1)}), bf16[2,768,512]{2,1,0:T(8,128)(2,1)}) %reduce-scatter.2.cloned.1.call-update) | async-done | bytes 1572880 | tf_op jit(solution)/shard_map/reduce_scatter | solution.py:43
  401.2 4.2 copy.28
  405.4 7.6 %all-to-all-start.1 = ((bf16[2,768,512]{2,0,1:T(2,128)(2,1)}), bf16[2,768,512]{2,0,1:T(2,128)(2,1)}, u32[]{:S(2)}, u32[]{:S(2)}) async-start(bf16[2,768,512]{2,0,1:T(2,128)(2,1)} %copy.28), calls=%async_computation.2 | async-start | bytes 3145728 | tf_op jit(solution)/shard_map/all_to_all | solution.py:45
  413.1 0.1 copy.30
  413.2 0.1 reshape.77
  413.3 6.8 %gather_fusion.2 = bf16[1024]{0:T(1024)(128)(2,1)S(1)} fusion(bf16[1536]{0:T(1024)(128)(2,1)S(1)} %reshape.77, s32[1024]{0:T(1024)S(1)} %broadcast_clamp_fusion), kind=kCustom, calls=%fused_computation.2 | custom fusion | bytes 8192 | tf_op jit(solution)/shard_map/gather | solution.py:53
  420.2 0.7 copy.32
  420.9 14.9 %all-to-all-done.1 = bf16[2,768,512]{2,0,1:T(2,128)(2,1)} async-done(((bf16[2,768,512]{2,0,1:T(2,128)(2,1)}), bf16[2,768,512]{2,0,1:T(2,128)(2,1)}, u32[]{:S(2)}, u32[]{:S(2)}) %all-to-all-start.1) | async-done | bytes 1572896 | tf_op jit(solution)/shard_map/all_to_all | solution.py:45
  435.8 2.9 copy.29
  438.7 6.7 %gather_fusion.1 = bf16[1024,512]{1,0:T(8,128)(2,1)} fusion(bf16[1536,512]{1,0:T(8,128)(2,1)} %bitcast.40, s32[1024]{0:T(1024)S(1)} %broadcast_clamp_fusion), kind=kCustom, calls=%fused_computation.1 | custom fusion | bytes 2101248 | tf_op jit(solution)/shard_map/gather | solution.py:48
  445.4 2.6 fusion
  (25 shorter events, 0.6 us)
Async XLA Ops:
  7.2 235.1 %copy-start = (bf16[2,192,4096]{2,1,0:T(8,128)(2,1)S(1)}, bf16[2,192,4096]{2,1,0:T(8,128)(2,1)}, u32[]{:S(2)}) copy-start(bf16[2,192,4096]{2,1,0:T(8,128)(2,1)} %param.11) | copy-start | bytes 9437188
  7.2 35.6 %copy-start.1 = (s32[128,8]{0,1:T(8,128)S(1)}, s32[128,8]{0,1:T(8,128)}, u32[]{:S(2)}) copy-start(s32[128,8]{0,1:T(8,128)} %param.10) | copy-start | bytes 12292
  7.2 40.4 %all-gather.4.cloned.1.call-start = ((), (), s32[]{:S(2)}) async-start(), calls=%async_computation.4 | async-start | bytes 1179648 | tf_op jit(solution)/shard_map/all_gather | solution.py:26
  7.9 393.3 %reduce-scatter.2.cloned.1.call-start = ((), (), s32[]{:S(2)}) async-start(), calls=%async_computation.5 | async-start | bytes 14155776 | tf_op jit(solution)/shard_map/reduce_scatter | solution.py:43
  291.9 113.5 %all-to-all-start.2 = ((bf16[2,32,24]{2,0,1:T(2,128)(2,1)}), bf16[2,32,24]{2,0,1:T(2,128)(2,1)S(1)}, u32[]{:S(2)}, u32[]{:S(2)}) async-start(bf16[2,32,24]{2,0,1:T(2,128)(2,1)} %copy.31), calls=%async_computation.3 | async-start | bytes 32768 | tf_op jit(solution)/shard_map/all_to_all | solution.py:46
  405.4 7.7 %copy-start.2 = (f32[128,8]{0,1:T(8,128)S(1)}, f32[128,8]{0,1:T(8,128)}, u32[]{:S(2)}) copy-start(f32[128,8]{0,1:T(8,128)} %param.9) | copy-start | bytes 12292
  405.4 30.4 %all-to-all-start.1 = ((bf16[2,768,512]{2,0,1:T(2,128)(2,1)}), bf16[2,768,512]{2,0,1:T(2,128)(2,1)}, u32[]{:S(2)}, u32[]{:S(2)}) async-start(bf16[2,768,512]{2,0,1:T(2,128)(2,1)} %copy.28), calls=%async_computation.2 | async-start | bytes 3145728 | tf_op jit(solution)/shard_map/all_to_all | solution.py:45
Sparse Core Ops, SparseCore 0:
  9.8 37.5 all-gather.3
  270.7 130.5 reduce-scatter.1
